TPU v7x, 32 devices: a whole 2x2x4 slice. The times are simulated.
32 devices in a mesh: hier: 8 (over y, x, core), col: 4 (over z).
Axes of the slice: x: 2, y: 2, z: 4, core: 2. Of those that a mesh axis runs over, the one named last changes fastest.
Arguments:
- densities: float32 [32, 2, 256, 256], P('hier', None, 'col'), may hold values from -6 to 6
- hamiltonian: float32 [256, 256], replicated, may hold values from -0.35355339 to 0.35355339, as said below
- couplings: float32 [2, 256, 256], replicated, may hold values from -0.088388348 to 0.088388348, as said below
- gamma: float32 [2], replicated, may hold values from 0.005 to 0.05
- coeff: float32 [2, 2], replicated, may hold values from -0.5 to 0.5
- node_count: int32 [8], replicated, may hold values from 2 to 4, as said below
Outputs:
- new_densities: float32 [32, 2, 256, 256], P('hier', None, 'col')
Inputs may be any that keep to these rules, and one draw needn't show every extreme that they name: `node_count`: at least one index of hier holds 4 nodes; every index holds 2 or more. `hamiltonian`: symmetric. `couplings`: each of the two matrices is symmetric.
All inputs are finite; a program needn't handle non-finite values.
Results may differ from a plain program's by a relative error of at most 0.00012.
Values sent between devices are 32-bit elements; how exact they have to be, the bound alone decides.
A program may use at most 64 MiB of HBM per device.

v0:
```python
import jax
import jax.numpy as jnp
from jax import lax
from jax.sharding import PartitionSpec as P

DEPTH2 = 2
step_size = 0.2


def passed_along(block, axis, distance):
    devices = range(lax.axis_size(axis))
    route = [(i - distance, i) for i in devices if i - distance in devices]
    return lax.ppermute(block, axis, route)


def hierarchy(node_count, device, slot):
    shards = node_count.shape[0]
    columns = jnp.arange(shards, dtype=jnp.int32)
    offsets = jnp.cumsum(node_count) - node_count
    live_total = jnp.sum(node_count) // DEPTH2 * DEPTH2

    def lookup(table, which):
        return jnp.sum(jnp.where(which[:, None] == columns[None, :], table[None, :], 0), axis=1)

    index = lookup(offsets, device) + slot
    live = (slot < lookup(node_count, device)) & (index < live_total)
    first = index // DEPTH2
    second = index % DEPTH2
    targets = (index + DEPTH2, index + 1, index - DEPTH2, index - 1)
    allowed = (
        live & (index + DEPTH2 < live_total),
        live & (second + 1 < DEPTH2),
        live & (first > 0),
        live & (second > 0),
    )
    found = []
    for target, valid in zip(targets, allowed):
        owner = jnp.sum((offsets[None, :] <= target[:, None]).astype(jnp.int32), axis=1) - 1
        within = target - lookup(offsets, owner)
        owner_count = lookup(node_count, owner)
        found.append((owner, within, valid, owner_count))
    return (live, first, second, found)


def combine(upward, downward, raise_w, lower_w, real, imag):
    rise = raise_w[:, None, None]
    fall = lower_w[:, None, None]
    part_re = rise * upward[:, 0] + fall * (real * downward[:, 0] - imag * downward[:, 1])
    part_im = rise * upward[:, 1] + fall * (real * downward[:, 1] + imag * downward[:, 0])
    return jnp.stack([part_re, part_im], axis=1)


def mixes(linked, levels, coeff, sign):
    result = []
    for mode in range(2):
        result.append(
            combine(
                linked[mode],
                linked[mode + 2],
                jnp.sqrt(levels[mode] + 1.0),
                jnp.sqrt(levels[mode]),
                coeff[mode, 0],
                sign * coeff[mode, 1],
            )
        )
    return result


def pick(wide, positions, masks):
    return [jnp.take(wide, positions[j], axis=0) * masks[j] for j in range(4)]


def tail_slots(block, start, half):
    return lax.dynamic_slice_in_dim(block, start, half, 0)


def slope(state, left_mat, right_mat, gamma, coeff, layout_info):
    alive, levels, positions, masks, tail_start = layout_info
    half = state.shape[0] // 2
    high = lax.Precision.HIGHEST
    own_cols = lax.all_to_all(state, "col", split_axis=3, concat_axis=2, tiled=True)
    lower = passed_along(
        (tail_slots(state, tail_start, half), tail_slots(own_cols, tail_start, half)), "hier", 1
    )
    upper = passed_along((state[:half], own_cols[:half]), "hier", -1)
    wide_rows = jnp.concatenate([lower[0], state, upper[0]], axis=0)
    wide_cols = jnp.concatenate([lower[1], own_cols, upper[1]], axis=0)
    rights = mixes(pick(wide_rows, positions, masks), levels, coeff, -1.0)
    lefts = mixes(pick(wide_cols, positions, masks), levels, coeff, 1.0)
    col_stack = jnp.concatenate([own_cols] + lefts, axis=2)
    right = jnp.einsum(
        "scij,jk->scik", jnp.concatenate([state] + rights, axis=3), right_mat, precision=high
    )
    left_cols = jnp.einsum("ij,scjk->scik", left_mat, col_stack, precision=high)
    left = lax.all_to_all(left_cols, "col", split_axis=2, concat_axis=3, tiled=True)
    comm = left - right
    damping = (levels[0] * gamma[0] + levels[1] * gamma[1])[:, None, None]
    out_re = comm[:, 1] - damping * state[:, 0]
    out_im = -comm[:, 0] - damping * state[:, 1]
    return jnp.stack([out_re, out_im], axis=1) * alive


def on_device(densities, hamiltonian, couplings, gamma, coeff, node_count):
    width = densities.shape[0]
    half = width // 2
    here = lax.axis_index("hier")
    device = jnp.full((width,), here, jnp.int32)
    slot = jnp.arange(width, dtype=jnp.int32)
    live, first, second, found = hierarchy(node_count, device, slot)
    own_count = jnp.sum(
        jnp.where(jnp.arange(node_count.shape[0], dtype=jnp.int32) == here, node_count, 0)
    )
    tail_start = own_count - half
    positions = []
    for o, w, v, c in found:
        place = jnp.where(
            o == here, half + w, jnp.where(o < here, w - (c - half), half + width + w)
        )
        positions.append(jnp.where(v, place, 0))
    masks = [v.astype(jnp.float32)[:, None, None, None] for o, w, v, c in found]
    levels = (first.astype(jnp.float32), second.astype(jnp.float32))
    alive = live.astype(jnp.float32)[:, None, None, None]
    layout_info = (alive, levels, positions, masks, tail_start)
    left_mat = jnp.concatenate([hamiltonian, couplings[0], couplings[1]], axis=1)
    right_mat = jnp.concatenate([hamiltonian, couplings[0], couplings[1]], axis=0)
    first_slope = slope(densities, left_mat, right_mat, gamma, coeff, layout_info)
    middle = densities + 0.5 * step_size * first_slope
    second_slope = slope(middle, left_mat, right_mat, gamma, coeff, layout_info)
    return densities + step_size * second_slope


def solution(mesh):
    placed = (P("hier", None, "col", None), P(), P(), P(), P(), P())
    return jax.shard_map(
        on_device,
        mesh=mesh,
        in_specs=placed,
        out_specs=P("hier", None, "col", None),
        check_vma=False,
    )
```

profile of v0, /device:TPU:3, one launch (start us, length us, event | category | flops | bytes accessed | tf_op | source)
XLA Modules:
  0.0 187.6 jit_solution(3273176700388385365)
XLA Ops:
  0.0 1.5 copy.27
  1.6 1.8 reshape.390
  3.3 4.7 %all-to-all-start = ((f32[4,1,32768]{2,1,0:T(1,128)}), f32[4,1,32768]{2,1,0:T(1,128)S(1)}, u32[]{:S(2)}, u32[]{:S(2)}) async-start(f32[4,1,32768]{2,1,0:T(1,128)} %reshape.390), calls=%async_computation | async-start | bytes 1048576 | tf_op jit(solution)/shard_map/all_to_all | solution.py:81
  10.3 4.0 %collective-permute-start.2 = (f32[2,2,64,256]{3,2,1,0:T(8,128)S(1)}, f32[2,2,64,256]{3,2,1,0:T(8,128)S(1)}, u32[]{:S(2)}, u32[]{:S(2)}) collective-permute-start(f32[2,2,64,256]{3,2,1,0:T(8,128)S(1)} %get-tuple-element.57), channel_id=1, source_target_pairs={{0,4},{4,8},{8,12},{12,16},{16,20},{20,24},{24,28},{1,5},{5,9},{9,... | collective-permute-start | bytes 786440 | tf_op jit(solution)/shard_map/ppermute | solution.py:13
  14.2 1.9 %collective-permute-start.3 = (f32[2,2,64,256]{3,2,1,0:T(8,128)S(1)}, f32[2,2,64,256]{3,2,1,0:T(8,128)S(1)}, u32[]{:S(2)}, u32[]{:S(2)}) collective-permute-start(f32[2,2,64,256]{3,2,1,0:T(8,128)S(1)} %get-tuple-element.56), channel_id=1, source_target_pairs={{4,0},{8,4},{12,8},{16,12},{20,16},{24,20},{28,24},{5,1},{9,5},{13... | collective-permute-start | bytes 786440 | tf_op jit(solution)/shard_map/ppermute | solution.py:13
  26.1 2.0 %reduce = f32[4,32768]{1,0:T(4,128)S(1)} reduce(f32[4,1,32768]{2,1,0:T(1,128)S(1)} %all-to-all-done, f32[]{:T(128)} %broadcast.622), dimensions={1}, to_apply=%all_to_all.52.reduce_sub_computation | reduce | bytes 1048580 | tf_op jit(solution)/shard_map/all_to_all | solution.py:81
  28.1 1.7 reshape.391
  29.8 1.9 %copy.44 = f32[4,2,64,4,64]{2,3,4,1,0:T(4,128)S(1)} copy(f32[4,2,64,4,64]{2,0,1,4,3:T(4,128)} %bitcast.69) | data formatting | bytes 1048576 | tf_op jit(solution)/shard_map/all_to_all | solution.py:81
  33.1 4.5 %collective-permute-start = (f32[2,2,256,64]{2,3,1,0:T(8,128)}, f32[2,2,256,64]{2,3,1,0:T(8,128)}, u32[]{:S(2)}, u32[]{:S(2)}) collective-permute-start(f32[2,2,256,64]{2,3,1,0:T(8,128)} %constant_dynamic-slice_fusion.2), channel_id=1, source_target_pairs={{0,4},{4,8},{8,12},{12,16},{16,20},{20,24},{24,28},{1,5},{5,9},{9,... | collective-permute-start | bytes 786440 | tf_op jit(solution)/shard_map/ppermute | solution.py:13
  37.7 2.0 %select_multiply_fusion.9 = f32[4,2,64,256]{3,2,1,0:T(8,128)} fusion(f32[4,2,64,256]{3,2,1,0:T(8,128)} %gather_fusion.6, f32[4]{0:T(128)S(1)} %get-tuple-element.73, pred[4]{0:T(512)(128)(4,1)S(1)} %get-tuple-element.68), kind=kLoop, calls=%fused_computation.82 | loop fusion | flops 262144 | bytes 1048596 | tf_op jit(solution)/shard_map/mul | solution.py:70
  41.8 1.4 slice.195
  43.3 1.9 %collective-permute-start.1 = (f32[2,2,256,64]{2,3,1,0:T(8,128)S(1)}, f32[2,2,256,64]{2,3,1,0:T(8,128)}, u32[]{:S(2)}, u32[]{:S(2)}) collective-permute-start(f32[2,2,256,64]{2,3,1,0:T(8,128)S(1)} %slice.195), channel_id=1, source_target_pairs={{4,0},{8,4},{12,8},{16,12},{20,16},{24,20},{28,24},{5,1},{9,5},{13... | collective-permute-start | bytes 786440 | tf_op jit(solution)/shard_map/ppermute | solution.py:13
  48.6 3.4 %collective-permute-done.1 = f32[2,2,256,64]{2,3,1,0:T(8,128)} collective-permute-done((f32[2,2,256,64]{2,3,1,0:T(8,128)S(1)}, f32[2,2,256,64]{2,3,1,0:T(8,128)}, u32[]{:S(2)}, u32[]{:S(2)}) %collective-permute-start.1) | collective-permute-done | bytes 262176 | tf_op jit(solution)/shard_map/ppermute | solution.py:13
  56.3 2.0 %select_multiply_fusion.13 = f32[4,2,256,64]{2,3,1,0:T(8,128)} fusion(f32[4,2,256,64]{2,3,1,0:T(8,128)} %gather_fusion.2, f32[4]{0:T(128)S(1)} %get-tuple-element.73, pred[4]{0:T(512)(128)(4,1)S(1)} %get-tuple-element.68), kind=kLoop, calls=%fused_computation.86 | loop fusion | flops 262144 | bytes 1048596 | tf_op jit(solution)/shard_map/mul | solution.py:70
  63.3 1.6 fusion.74
  65.0 1.4 fusion.43
  67.2 1.9 %reshape.392 = f32[4,1,32768]{2,1,0:T(1,128)} reshape(f32[256,4,2,64]{3,2,1,0:T(2,128)S(1)} %bitcast.65) | data formatting | bytes 1048576
  69.1 4.9 %all-to-all-start.1 = ((f32[4,1,32768]{2,1,0:T(1,128)}), f32[4,1,32768]{2,1,0:T(1,128)}, u32[]{:S(2)}, u32[]{:S(2)}) async-start(f32[4,1,32768]{2,1,0:T(1,128)} %reshape.392), calls=%async_computation.1 | async-start | bytes 1048576 | tf_op jit(solution)/shard_map/all_to_all | solution.py:95
  76.8 1.5 fusion.68
  78.3 1.6 fusion.70
  79.9 6.6 %all-to-all-done.1 = f32[4,1,32768]{2,1,0:T(1,128)} async-done(((f32[4,1,32768]{2,1,0:T(1,128)}), f32[4,1,32768]{2,1,0:T(1,128)}, u32[]{:S(2)}, u32[]{:S(2)}) %all-to-all-start.1) | async-done | bytes 524320 | tf_op jit(solution)/shard_map/all_to_all | solution.py:95
  86.5 3.0 %reduce.1 = f32[4,32768]{1,0:T(4,128)S(1)} reduce(f32[4,1,32768]{2,1,0:T(1,128)} %all-to-all-done.1, f32[]{:T(128)} %broadcast.622), dimensions={1}, to_apply=%all_to_all.56.reduce_sub_computation | reduce | bytes 1048580 | tf_op jit(solution)/shard_map/all_to_all | solution.py:95
  92.2 2.4 %fusion.49 = f32[4,2,64,256]{3,2,1,0:T(8,128)S(1)} fusion(f32[4,2,64,256]{3,2,1,0:T(8,128)S(1)} %all_to_all.59, f32[4,1,64,256]{3,2,1,0:T(8,128)S(1)} %copy-done.29, f32[4,1,64,256]{3,2,1,0:T(8,128)S(1)} %copy-done.28, f32[4,1,64,256]{3,2,1,0:T(8,128)} %get-tuple-element.43, f32[4,1,64,256]{3,2,1,0:T(8,128)S(1)} %copy-done.30, ...), kind=kOutput, calls=%fused_computation.59 | convolution fusion | flops 1210056704 | bytes 3407872 | tf_op jit(solution)/shard_map/scij,jk->scik/dot_general | solution.py:91
  95.6 1.9 %reshape.394 = f32[4,1,32768]{2,1,0:T(1,128)} reshape(f32[256,4,2,64]{3,2,1,0:T(2,128)S(1)} %bitcast.68) | data formatting | bytes 1048576
  97.5 3.5 %all-to-all-start.2 = ((f32[4,1,32768]{2,1,0:T(1,128)}), f32[4,1,32768]{2,1,0:T(1,128)S(1)}, u32[]{:S(2)}, u32[]{:S(2)}) async-start(f32[4,1,32768]{2,1,0:T(1,128)} %reshape.394), calls=%async_computation.2 | async-start | bytes 1048576 | tf_op jit(solution)/shard_map/all_to_all | solution.py:81
  101.1 1.9 %collective-permute-start.7 = (f32[2,2,64,256]{3,2,1,0:T(8,128)S(1)}, f32[2,2,64,256]{3,2,1,0:T(8,128)S(1)}, u32[]{:S(2)}, u32[]{:S(2)}) collective-permute-start(f32[2,2,64,256]{3,2,1,0:T(8,128)S(1)} %get-tuple-element.55), channel_id=1, source_target_pairs={{4,0},{8,4},{12,8},{16,12},{20,16},{24,20},{28,24},{5,1},{9,5},{13... | collective-permute-start | bytes 786440 | tf_op jit(solution)/shard_map/ppermute | solution.py:13
  103.0 4.5 %collective-permute-start.6 = (f32[2,2,64,256]{3,2,1,0:T(8,128)S(1)}, f32[2,2,64,256]{3,2,1,0:T(8,128)S(1)}, u32[]{:S(2)}, u32[]{:S(2)}) collective-permute-start(f32[2,2,64,256]{3,2,1,0:T(8,128)S(1)} %get-tuple-element.54), channel_id=1, source_target_pairs={{0,4},{4,8},{8,12},{12,16},{16,20},{20,24},{24,28},{1,5},{5,9},{9,... | collective-permute-start | bytes 786440 | tf_op jit(solution)/shard_map/ppermute | solution.py:13
  107.5 3.4 %collective-permute-done.7 = f32[2,2,64,256]{3,2,1,0:T(8,128)S(1)} collective-permute-done((f32[2,2,64,256]{3,2,1,0:T(8,128)S(1)}, f32[2,2,64,256]{3,2,1,0:T(8,128)S(1)}, u32[]{:S(2)}, u32[]{:S(2)}) %collective-permute-start.7) | collective-permute-done | bytes 262176 | tf_op jit(solution)/shard_map/ppermute | solution.py:13
  112.4 3.5 %all-to-all-done.2 = f32[4,1,32768]{2,1,0:T(1,128)S(1)} async-done(((f32[4,1,32768]{2,1,0:T(1,128)}), f32[4,1,32768]{2,1,0:T(1,128)S(1)}, u32[]{:S(2)}, u32[]{:S(2)}) %all-to-all-start.2) | async-done | bytes 524320 | tf_op jit(solution)/shard_map/all_to_all | solution.py:81
  115.9 2.0 %reduce.2 = f32[4,32768]{1,0:T(4,128)S(1)} reduce(f32[4,1,32768]{2,1,0:T(1,128)S(1)} %all-to-all-done.2, f32[]{:T(128)} %broadcast.622), dimensions={1}, to_apply=%all_to_all.60.reduce_sub_computation | reduce | bytes 1048580 | tf_op jit(solution)/shard_map/all_to_all | solution.py:81
  118.0 1.8 reshape.395
  119.8 1.9 %copy.42 = f32[4,2,64,4,64]{2,3,4,1,0:T(4,128)S(1)} copy(f32[4,2,64,4,64]{2,1,0,4,3:T(2,128)} %bitcast.72) | data formatting | bytes 1048576 | tf_op jit(solution)/shard_map/all_to_all | solution.py:81
  123.1 1.7 constant_dynamic-slice_fusion
  124.8 3.7 %collective-permute-start.4 = (f32[2,2,256,64]{2,3,1,0:T(8,128)}, f32[2,2,256,64]{2,3,1,0:T(8,128)}, u32[]{:S(2)}, u32[]{:S(2)}) collective-permute-start(f32[2,2,256,64]{2,3,1,0:T(8,128)} %constant_dynamic-slice_fusion), channel_id=1, source_target_pairs={{0,4},{4,8},{8,12},{12,16},{16,20},{20,24},{24,28},{1,5},{5,9},{9,... | collective-permute-start | bytes 786440 | tf_op jit(solution)/shard_map/ppermute | solution.py:13
  128.4 2.0 %select_multiply_fusion.1 = f32[4,2,64,256]{3,2,1,0:T(8,128)} fusion(f32[4,2,64,256]{3,2,1,0:T(8,128)} %gather_fusion.14, f32[4]{0:T(128)S(1)} %get-tuple-element.73, pred[4]{0:T(512)(128)(4,1)S(1)} %get-tuple-element.68), kind=kLoop, calls=%fused_computation.74 | loop fusion | flops 262144 | bytes 1048596 | tf_op jit(solution)/shard_map/mul | solution.py:70
  132.6 1.4 slice.226
  134.0 1.9 %collective-permute-start.5 = (f32[2,2,256,64]{2,3,1,0:T(8,128)S(1)}, f32[2,2,256,64]{2,3,1,0:T(8,128)}, u32[]{:S(2)}, u32[]{:S(2)}) collective-permute-start(f32[2,2,256,64]{2,3,1,0:T(8,128)S(1)} %slice.226), channel_id=1, source_target_pairs={{4,0},{8,4},{12,8},{16,12},{20,16},{24,20},{28,24},{5,1},{9,5},{13... | collective-permute-start | bytes 786440 | tf_op jit(solution)/shard_map/ppermute | solution.py:13
  140.3 2.4 %collective-permute-done.5 = f32[2,2,256,64]{2,3,1,0:T(8,128)} collective-permute-done((f32[2,2,256,64]{2,3,1,0:T(8,128)S(1)}, f32[2,2,256,64]{2,3,1,0:T(8,128)}, u32[]{:S(2)}, u32[]{:S(2)}) %collective-permute-start.5) | collective-permute-done | bytes 262176 | tf_op jit(solution)/shard_map/ppermute | solution.py:13
  153.1 1.6 fusion.65
  154.7 2.2 %fusion.40 = f32[4,2,256,64]{2,3,1,0:T(8,128)} fusion(f32[4,1,256,64]{2,3,1,0:T(8,128)S(1)} %get-tuple-element.41, f32[4,1,256,64]{2,3,1,0:T(8,128)S(1)} %get-tuple-element.40, f32[4,1,256,64]{2,3,1,0:T(8,128)S(1)} %get-tuple-element.39, f32[4,1,256,64]{2,3,1,0:T(8,128)S(1)} %get-tuple-element.38, f32[4,2,256,64]{2,3,1,0:T(8,128)S(1)} %copy-done.6, ...), kind=kOutput, calls=%fused_computation.56 | convolution fusion | flops 1209925632 | bytes 2883584 | tf_op jit(solution)/shard_map/ij,scjk->scik/dot_general | solution.py:94
  157.0 1.7 copy.33
  158.6 1.9 %reshape.396 = f32[4,1,32768]{2,1,0:T(1,128)} reshape(f32[256,4,2,64]{3,2,1,0:T(2,128)S(1)} %bitcast.66) | data formatting | bytes 1048576
  160.5 4.3 %all-to-all-start.3 = ((f32[4,1,32768]{2,1,0:T(1,128)}), f32[4,1,32768]{2,1,0:T(1,128)}, u32[]{:S(2)}, u32[]{:S(2)}) async-start(f32[4,1,32768]{2,1,0:T(1,128)} %reshape.396), calls=%async_computation.3 | async-start | bytes 1048576 | tf_op jit(solution)/shard_map/all_to_all | solution.py:95
  168.3 1.6 fusion.59
  169.9 1.6 fusion.61
  171.5 6.9 %all-to-all-done.3 = f32[4,1,32768]{2,1,0:T(1,128)} async-done(((f32[4,1,32768]{2,1,0:T(1,128)}), f32[4,1,32768]{2,1,0:T(1,128)}, u32[]{:S(2)}, u32[]{:S(2)}) %all-to-all-start.3) | async-done | bytes 524320 | tf_op jit(solution)/shard_map/all_to_all | solution.py:95
  178.4 3.0 %reduce.3 = f32[4,32768]{1,0:T(4,128)S(1)} reduce(f32[4,1,32768]{2,1,0:T(1,128)} %all-to-all-done.3, f32[]{:T(128)} %broadcast.622), dimensions={1}, to_apply=%all_to_all.64.reduce_sub_computation | reduce | bytes 1048580 | tf_op jit(solution)/shard_map/all_to_all | solution.py:95
  183.9 2.6 %fusion.46 = f32[4,2,64,256]{3,2,1,0:T(8,128)S(1)} fusion(f32[4,2,64,256]{3,2,1,0:T(8,128)S(1)} %all_to_all.67, f32[4,1,64,256]{3,2,1,0:T(8,128)} %get-tuple-element.37, f32[4,1,64,256]{3,2,1,0:T(8,128)S(1)} %copy-done.27, f32[4,1,64,256]{3,2,1,0:T(8,128)} %get-tuple-element.35, f32[4,1,64,256]{3,2,1,0:T(8,128)} %get-tuple-element.34, ...), kind=kOutput, calls=%fused_computation.58 | convolution fusion | flops 1210056704 | bytes 3407872 | tf_op jit(solution)/shard_map/scij,jk->scik/dot_general | solution.py:91
  (161 shorter events, 57.3 us)
Async XLA Ops:
  1.5 6.5 %copy-start.31 = (s32[8]{0:T(128)S(1)}, s32[8]{0:T(128)}, u32[]{:S(2)}) copy-start(s32[8]{0:T(128)} %param.15) | copy-start | bytes 100
  1.6 8.6 %copy-start = (f32[4,2,64,256]{3,2,1,0:T(8,128)S(1)}, f32[4,2,64,256]{3,2,1,0:T(8,128)}, u32[]{:S(2)}) copy-start(f32[4,2,64,256]{3,2,1,0:T(8,128)} %param.10) | copy-start | bytes 1572868
  3.3 15.4 %copy-start.33 = (f32[2]{0:T(128)S(1)}, f32[2]{0:T(128)}, u32[]{:S(2)}) copy-start(f32[2]{0:T(128)} %param.13) | copy-start | bytes 28
  3.3 17.9 %copy-start.20 = (f32[2,256,256]{2,1,0:T(8,128)S(1)}, f32[2,256,256]{2,1,0:T(8,128)}, u32[]{:S(2)}) copy-start(f32[2,256,256]{2,1,0:T(8,128)} %param.12) | copy-start | bytes 1572868
  3.3 22.3 %all-to-all-start = ((f32[4,1,32768]{2,1,0:T(1,128)}), f32[4,1,32768]{2,1,0:T(1,128)S(1)}, u32[]{:S(2)}, u32[]{:S(2)}) async-start(f32[4,1,32768]{2,1,0:T(1,128)} %reshape.390), calls=%async_computation | async-start | bytes 1048576 | tf_op jit(solution)/shard_map/all_to_all | solution.py:81
  10.2 11.9 %copy-start.32 = (f32[2,2]{1,0:T(2,128)S(1)}, f32[2,2]{1,0:T(2,128)}, u32[]{:S(2)}) copy-start(f32[2,2]{1,0:T(2,128)} %param.14) | copy-start | bytes 52
  10.3 13.8 %collective-permute-start.2 = (f32[2,2,64,256]{3,2,1,0:T(8,128)S(1)}, f32[2,2,64,256]{3,2,1,0:T(8,128)S(1)}, u32[]{:S(2)}, u32[]{:S(2)}) collective-permute-start(f32[2,2,64,256]{3,2,1,0:T(8,128)S(1)} %get-tuple-element.57), channel_id=1, source_target_pairs={{0,4},{4,8},{8,12},{12,16},{16,20},{20,24},{24,28},{1,5},{5,9},{9,... | collective-permute-start | bytes 786440 | tf_op jit(solution)/shard_map/ppermute | solution.py:13
  14.2 10.0 %collective-permute-start.3 = (f32[2,2,64,256]{3,2,1,0:T(8,128)S(1)}, f32[2,2,64,256]{3,2,1,0:T(8,128)S(1)}, u32[]{:S(2)}, u32[]{:S(2)}) collective-permute-start(f32[2,2,64,256]{3,2,1,0:T(8,128)S(1)} %get-tuple-element.56), channel_id=1, source_target_pairs={{4,0},{8,4},{12,8},{16,12},{20,16},{24,20},{28,24},{5,1},{9,5},{13... | collective-permute-start | bytes 786440 | tf_op jit(solution)/shard_map/ppermute | solution.py:13
  32.4 16.2 %copy-start.7 = (f32[4,2,256,64]{2,3,1,0:T(8,128)}, f32[4,2,256,64]{2,3,1,0:T(8,128)S(1)}, u32[]{:S(2)}) copy-start(f32[4,2,256,64]{2,3,1,0:T(8,128)S(1)} %all_to_all.55) | copy-start | bytes 1572868
  33.1 14.4 %collective-permute-start = (f32[2,2,256,64]{2,3,1,0:T(8,128)}, f32[2,2,256,64]{2,3,1,0:T(8,128)}, u32[]{:S(2)}, u32[]{:S(2)}) collective-permute-start(f32[2,2,256,64]{2,3,1,0:T(8,128)} %constant_dynamic-slice_fusion.2), channel_id=1, source_target_pairs={{0,4},{4,8},{8,12},{12,16},{16,20},{20,24},{24,28},{1,5},{5,9},{9,... | collective-permute-start | bytes 786440 | tf_op jit(solution)/shard_map/ppermute | solution.py:13
  41.8 3.4 %copy-start.18 = (f32[4,2,64,256]{3,2,1,0:T(8,128)S(1)}, f32[4,2,64,256]{3,2,1,0:T(8,128)}, u32[]{:S(2)}) copy-start(f32[4,2,64,256]{3,2,1,0:T(8,128)} %gather_fusion.7) | copy-start | bytes 1572868
  43.3 8.7 %collective-permute-start.1 = (f32[2,2,256,64]{2,3,1,0:T(8,128)S(1)}, f32[2,2,256,64]{2,3,1,0:T(8,128)}, u32[]{:S(2)}, u32[]{:S(2)}) collective-permute-start(f32[2,2,256,64]{2,3,1,0:T(8,128)S(1)} %slice.195), channel_id=1, source_target_pairs={{4,0},{8,4},{12,8},{16,12},{20,16},{24,20},{28,24},{5,1},{9,5},{13... | collective-permute-start | bytes 786440 | tf_op jit(solution)/shard_map/ppermute | solution.py:13
  56.3 2.0 %copy-start.5 = (f32[4,2,256,64]{2,3,1,0:T(8,128)S(1)}, f32[4,2,256,64]{2,3,1,0:T(8,128)}, u32[]{:S(2)}) copy-start(f32[4,2,256,64]{2,3,1,0:T(8,128)} %gather_fusion.3) | copy-start | bytes 1572868
  60.6 1.0 copy-start.4
  60.6 1.2 copy-start.14
  60.6 1.4 copy-start.15
  63.3 1.6 copy-start.8
  63.3 1.6 copy-start.21
  63.3 1.6 copy-start.23
  63.3 1.6 copy-start.34
  69.1 4.9 %copy-start.17 = (f32[4,2,64,256]{3,2,1,0:T(8,128)S(1)}, f32[4,2,64,256]{3,2,1,0:T(8,128)}, u32[]{:S(2)}) copy-start(f32[4,2,64,256]{3,2,1,0:T(8,128)} %gather_fusion.4) | copy-start | bytes 1572868
  69.1 17.4 %all-to-all-start.1 = ((f32[4,1,32768]{2,1,0:T(1,128)}), f32[4,1,32768]{2,1,0:T(1,128)}, u32[]{:S(2)}, u32[]{:S(2)}) async-start(f32[4,1,32768]{2,1,0:T(1,128)} %reshape.392), calls=%async_computation.1 | async-start | bytes 1048576 | tf_op jit(solution)/shard_map/all_to_all | solution.py:95
  74.2 2.6 %copy-start.11 = (f32[4,2,64,256]{3,2,1,0:T(8,128)S(1)}, f32[4,2,64,256]{3,2,1,0:T(8,128)}, u32[]{:S(2)}) copy-start(f32[4,2,64,256]{3,2,1,0:T(8,128)} %select_multiply_fusion.9) | copy-start | bytes 1572868
  74.2 2.6 %copy-start.12 = (f32[4,2,64,256]{3,2,1,0:T(8,128)S(1)}, f32[4,2,64,256]{3,2,1,0:T(8,128)}, u32[]{:S(2)}) copy-start(f32[4,2,64,256]{3,2,1,0:T(8,128)} %select_multiply_fusion.8) | copy-start | bytes 1572868
  91.0 1.0 copy-start.24
  91.0 1.0 copy-start.28
  91.0 1.1 copy-start.29
  91.0 1.2 copy-start.30
  97.5 18.4 %all-to-all-start.2 = ((f32[4,1,32768]{2,1,0:T(1,128)}), f32[4,1,32768]{2,1,0:T(1,128)S(1)}, u32[]{:S(2)}, u32[]{:S(2)}) async-start(f32[4,1,32768]{2,1,0:T(1,128)} %reshape.394), calls=%async_computation.2 | async-start | bytes 1048576 | tf_op jit(solution)/shard_map/all_to_all | solution.py:81
  101.1 9.8 %collective-permute-start.7 = (f32[2,2,64,256]{3,2,1,0:T(8,128)S(1)}, f32[2,2,64,256]{3,2,1,0:T(8,128)S(1)}, u32[]{:S(2)}, u32[]{:S(2)}) collective-permute-start(f32[2,2,64,256]{3,2,1,0:T(8,128)S(1)} %get-tuple-element.55), channel_id=1, source_target_pairs={{4,0},{8,4},{12,8},{16,12},{20,16},{24,20},{28,24},{5,1},{9,5},{13... | collective-permute-start | bytes 786440 | tf_op jit(solution)/shard_map/ppermute | solution.py:13
  103.0 7.9 %collective-permute-start.6 = (f32[2,2,64,256]{3,2,1,0:T(8,128)S(1)}, f32[2,2,64,256]{3,2,1,0:T(8,128)S(1)}, u32[]{:S(2)}, u32[]{:S(2)}) collective-permute-start(f32[2,2,64,256]{3,2,1,0:T(8,128)S(1)} %get-tuple-element.54), channel_id=1, source_target_pairs={{0,4},{4,8},{8,12},{12,16},{16,20},{20,24},{24,28},{1,5},{5,9},{9,... | collective-permute-start | bytes 786440 | tf_op jit(solution)/shard_map/ppermute | solution.py:13
  124.8 13.5 %collective-permute-start.4 = (f32[2,2,256,64]{2,3,1,0:T(8,128)}, f32[2,2,256,64]{2,3,1,0:T(8,128)}, u32[]{:S(2)}, u32[]{:S(2)}) collective-permute-start(f32[2,2,256,64]{2,3,1,0:T(8,128)} %constant_dynamic-slice_fusion), channel_id=1, source_target_pairs={{0,4},{4,8},{8,12},{12,16},{16,20},{20,24},{24,28},{1,5},{5,9},{9,... | collective-permute-start | bytes 786440 | tf_op jit(solution)/shard_map/ppermute | solution.py:13
  132.6 3.4 %copy-start.19 = (f32[4,2,64,256]{3,2,1,0:T(8,128)S(1)}, f32[4,2,64,256]{3,2,1,0:T(8,128)}, u32[]{:S(2)}) copy-start(f32[4,2,64,256]{3,2,1,0:T(8,128)} %gather_fusion.15) | copy-start | bytes 1572868
  134.0 8.7 %collective-permute-start.5 = (f32[2,2,256,64]{2,3,1,0:T(8,128)S(1)}, f32[2,2,256,64]{2,3,1,0:T(8,128)}, u32[]{:S(2)}, u32[]{:S(2)}) collective-permute-start(f32[2,2,256,64]{2,3,1,0:T(8,128)S(1)} %slice.226), channel_id=1, source_target_pairs={{4,0},{8,4},{12,8},{16,12},{20,16},{24,20},{28,24},{5,1},{9,5},{13... | collective-permute-start | bytes 786440 | tf_op jit(solution)/shard_map/ppermute | solution.py:13
  149.3 1.3 copy-start.1
  149.3 1.4 copy-start.2
  150.5 1.1 copy-start.3
  153.0 1.6 copy-start.6
  153.1 1.6 copy-start.22
  153.1 1.6 copy-start.25
  153.1 1.6 copy-start.35
  160.5 4.3 %copy-start.16 = (f32[4,2,64,256]{3,2,1,0:T(8,128)S(1)}, f32[4,2,64,256]{3,2,1,0:T(8,128)}, u32[]{:S(2)}) copy-start(f32[4,2,64,256]{3,2,1,0:T(8,128)} %gather_fusion.12) | copy-start | bytes 1572868
  160.5 17.9 %all-to-all-start.3 = ((f32[4,1,32768]{2,1,0:T(1,128)}), f32[4,1,32768]{2,1,0:T(1,128)}, u32[]{:S(2)}, u32[]{:S(2)}) async-start(f32[4,1,32768]{2,1,0:T(1,128)} %reshape.396), calls=%async_computation.3 | async-start | bytes 1048576 | tf_op jit(solution)/shard_map/all_to_all | solution.py:95
  165.7 2.5 %copy-start.9 = (f32[4,2,64,256]{3,2,1,0:T(8,128)S(1)}, f32[4,2,64,256]{3,2,1,0:T(8,128)}, u32[]{:S(2)}) copy-start(f32[4,2,64,256]{3,2,1,0:T(8,128)} %select_multiply_fusion.1) | copy-start | bytes 1572868
  165.7 2.6 %copy-start.10 = (f32[4,2,64,256]{3,2,1,0:T(8,128)S(1)}, f32[4,2,64,256]{3,2,1,0:T(8,128)}, u32[]{:S(2)}) copy-start(f32[4,2,64,256]{3,2,1,0:T(8,128)} %select_multiply_fusion) | copy-start | bytes 1572868
  168.3 1.6 copy-start.13
  182.9 1.0 copy-start.26
  182.9 1.0 copy-start.27
where the time goes:
time: 189 us; the launch traced here: 188 us
  local copies, waits for them, and re-layouts  64.8 us (34%)
  starting transfers between devices  41.8 us (22%)
  other arithmetic  40.4 us (21%)
  waiting for transfers between devices  26.2 us (14%)
  matrix products  8.67 us (5%)
  between operations  5.74 us (3%)
    ppermute x8, starting transfers between devices, passed_along(): return lax.ppermute(block, axis, route)  24.4 us
    gather x16, local copies, waits for them, and re-layouts, pick(): return [jnp.take(wide, positions[j], axis=0) * masks[j] for j in range(4)]  21.4 us
    unnamed x87, local copies, waits for them, and re-layouts  20.2 us
    mul x16, other arithmetic, pick(): return [jnp.take(wide, positions[j], axis=0) * masks[j] for j in range(4)]  13.8 us
    all_to_all x2, waiting for transfers between devices, slope(): lax.all_to_all(left_cols, 'col', split_axis=2, concat_axis=3, tiled=True)  13.5 us
    add x8, other arithmetic, combine(): rise * upward[:, 0] + fall * (real * downward[:, 0] - imag * downward[:, 1])  12.2 us
    all_to_all x2, starting transfers between devices, slope(): lax.all_to_all(left_cols, 'col', split_axis=2, concat_axis=3, tiled=True)  9.21 us
    ppermute x8, waiting for transfers between devices, passed_along(): return lax.ppermute(block, axis, route)  9.18 us
  transfers between devices with their start and end apart: 12, of which 6 were waited for; matrix products, arithmetic and copies ran while one was open for 21% of the time, Pallas kernels for 0%

commit v1 on v0

--- a/solution.py
+++ b/solution.py
@@ -78,7 +78,10 @@
     alive, levels, positions, masks, tail_start = layout_info
     half = state.shape[0] // 2
     high = lax.Precision.HIGHEST
-    own_cols = lax.all_to_all(state, "col", split_axis=3, concat_axis=2, tiled=True)
+    own_cols = jnp.concatenate(
+        lax.all_to_all(jnp.stack(jnp.split(state, lax.axis_size("col"), axis=3)), "col", 0, 0),
+        axis=2,
+    )
     lower = passed_along(
         (tail_slots(state, tail_start, half), tail_slots(own_cols, tail_start, half)), "hier", 1
     )

time: 189 us -> 190 us (level)
    reshape x0 -> x4, local copies, waits for them, and re-layouts: none -> 7.12 us  [slope(): jnp.concatenate(lax.all_to_all(jnp.stack(jnp.split(state, lax.axis_size('...]
    all_to_all x5 -> x1, local copies, waits for them, and re-layouts: 6.31 us -> 0.59 us  [slope(): lax.all_to_all(jnp.stack(jnp.split(state, lax.axis_size('col'), axis=3)),...]
    unnamed x87 -> x86, local copies, waits for them, and re-layouts: 20.2 us -> 16.5 us
    slice x5 -> x7, local copies, waits for them, and re-layouts: 4.56 us -> 5.04 us  [slope(): upper = passed_along((state[:half], own_cols[:half]), 'hier', -1)]
where the time goes in v1:
time: 190 us; the launch traced here: 188 us
  local copies, waits for them, and re-layouts  63.8 us (34%)
  starting transfers between devices  41.8 us (22%)
  other arithmetic  41.7 us (22%)
  waiting for transfers between devices  26.2 us (14%)
  matrix products  8.67 us (5%)
  between operations  5.93 us (3%)
    ppermute x8, starting transfers between devices, passed_along(): return lax.ppermute(block, axis, route)  24.4 us
    gather x16, local copies, waits for them, and re-layouts, pick(): return [jnp.take(wide, positions[j], axis=0) * masks[j] for j in range(4)]  21.4 us
    unnamed x86, local copies, waits for them, and re-layouts  16.5 us
    mul x16, other arithmetic, pick(): return [jnp.take(wide, positions[j], axis=0) * masks[j] for j in range(4)]  13.9 us
    all_to_all x2, waiting for transfers between devices, slope(): lax.all_to_all(left_cols, 'col', split_axis=2, concat_axis=3, tiled=True)  13.8 us
    add x8, other arithmetic, combine(): rise * upward[:, 0] + fall * (real * downward[:, 0] - imag * downward[:, 1])  11.9 us
    all_to_all x2, starting transfers between devices, slope(): lax.all_to_all(left_cols, 'col', split_axis=2, concat_axis=3, tiled=True)  9.21 us
    ppermute x8, waiting for transfers between devices, passed_along(): return lax.ppermute(block, axis, route)  8.95 us
  transfers between devices with their start and end apart: 12, of which 6 were waited for; matrix products, arithmetic and copies ran while one was open for 21% of the time, Pallas kernels for 0%

profile of v1, /device:TPU:3, one launch (start us, length us, event | category | flops | bytes accessed | tf_op | source)
XLA Modules:
  0.0 188.2 jit_solution(12794123460663514551)
XLA Ops:
  0.0 1.4 slice_bitcast_fusion.9
  1.5 1.4 reshape.406
  3.0 4.7 %all-to-all-start = ((f32[4,1,32768]{2,1,0:T(1,128)}), f32[4,1,32768]{2,1,0:T(1,128)S(1)}, u32[]{:S(2)}, u32[]{:S(2)}) async-start(f32[4,1,32768]{2,1,0:T(1,128)} %reshape.406), calls=%async_computation | async-start | bytes 1048576 | tf_op jit(solution)/shard_map/all_to_all | solution.py:82
  9.9 4.0 %collective-permute-start.2 = (f32[2,2,64,256]{3,2,1,0:T(8,128)S(1)}, f32[2,2,64,256]{3,2,1,0:T(8,128)S(1)}, u32[]{:S(2)}, u32[]{:S(2)}) collective-permute-start(f32[2,2,64,256]{3,2,1,0:T(8,128)S(1)} %get-tuple-element.61), channel_id=1, source_target_pairs={{0,4},{4,8},{8,12},{12,16},{16,20},{20,24},{24,28},{1,5},{5,9},{9,... | collective-permute-start | bytes 786440 | tf_op jit(solution)/shard_map/ppermute | solution.py:13
  13.9 1.9 %collective-permute-start.3 = (f32[2,2,64,256]{3,2,1,0:T(8,128)S(1)}, f32[2,2,64,256]{3,2,1,0:T(8,128)S(1)}, u32[]{:S(2)}, u32[]{:S(2)}) collective-permute-start(f32[2,2,64,256]{3,2,1,0:T(8,128)S(1)} %get-tuple-element.60), channel_id=1, source_target_pairs={{4,0},{8,4},{12,8},{16,12},{20,16},{24,20},{28,24},{5,1},{9,5},{13... | collective-permute-start | bytes 786440 | tf_op jit(solution)/shard_map/ppermute | solution.py:13
  26.1 2.2 %reduce = f32[4,32768]{1,0:T(4,128)S(1)} reduce(f32[4,1,32768]{2,1,0:T(1,128)S(1)} %all-to-all-done, f32[]{:T(128)} %broadcast.622), dimensions={1}, to_apply=%all_to_all.32.reduce_sub_computation | reduce | bytes 1048580 | tf_op jit(solution)/shard_map/all_to_all | solution.py:82
  30.1 1.8 reshape.223
  32.7 4.5 %collective-permute-start = (f32[2,2,256,64]{2,3,1,0:T(8,128)}, f32[2,2,256,64]{2,3,1,0:T(8,128)}, u32[]{:S(2)}, u32[]{:S(2)}) collective-permute-start(f32[2,2,256,64]{2,3,1,0:T(8,128)} %constant_dynamic-slice_fusion.2), channel_id=1, source_target_pairs={{0,4},{4,8},{8,12},{12,16},{16,20},{20,24},{24,28},{1,5},{5,9},{9,... | collective-permute-start | bytes 786440 | tf_op jit(solution)/shard_map/ppermute | solution.py:13
  37.3 2.0 %select_multiply_fusion.9 = f32[4,2,64,256]{3,2,1,0:T(8,128)} fusion(f32[4,2,64,256]{3,2,1,0:T(8,128)} %gather_fusion.6, f32[4]{0:T(128)S(1)} %get-tuple-element.81, pred[4]{0:T(512)(128)(4,1)S(1)} %get-tuple-element.76), kind=kLoop, calls=%fused_computation.82 | loop fusion | flops 262144 | bytes 1048596 | tf_op jit(solution)/shard_map/mul | solution.py:70
  43.1 1.9 %collective-permute-start.1 = (f32[2,2,256,64]{2,3,1,0:T(8,128)S(1)}, f32[2,2,256,64]{2,3,1,0:T(8,128)}, u32[]{:S(2)}, u32[]{:S(2)}) collective-permute-start(f32[2,2,256,64]{2,3,1,0:T(8,128)S(1)} %slice.195), channel_id=1, source_target_pairs={{4,0},{8,4},{12,8},{16,12},{20,16},{24,20},{28,24},{5,1},{9,5},{13... | collective-permute-start | bytes 786440 | tf_op jit(solution)/shard_map/ppermute | solution.py:13
  46.0 1.4 gather_fusion.4
  48.4 3.4 %collective-permute-done.1 = f32[2,2,256,64]{2,3,1,0:T(8,128)} collective-permute-done((f32[2,2,256,64]{2,3,1,0:T(8,128)S(1)}, f32[2,2,256,64]{2,3,1,0:T(8,128)}, u32[]{:S(2)}, u32[]{:S(2)}) %collective-permute-start.1) | collective-permute-done | bytes 262176 | tf_op jit(solution)/shard_map/ppermute | solution.py:13
  56.2 2.0 %select_multiply_fusion.13 = f32[4,2,256,64]{2,3,1,0:T(8,128)} fusion(f32[4,2,256,64]{2,3,1,0:T(8,128)} %gather_fusion.2, f32[4]{0:T(128)S(1)} %get-tuple-element.81, pred[4]{0:T(512)(128)(4,1)S(1)} %get-tuple-element.76), kind=kLoop, calls=%fused_computation.86 | loop fusion | flops 262144 | bytes 1048596 | tf_op jit(solution)/shard_map/mul | solution.py:70
  63.3 1.4 fusion.74
  64.8 1.4 fusion.43
  67.0 1.9 %reshape.408 = f32[4,1,32768]{2,1,0:T(1,128)} reshape(f32[256,4,2,64]{3,2,1,0:T(2,128)S(1)} %bitcast.71) | data formatting | bytes 1048576
  68.9 4.9 %all-to-all-start.1 = ((f32[4,1,32768]{2,1,0:T(1,128)}), f32[4,1,32768]{2,1,0:T(1,128)}, u32[]{:S(2)}, u32[]{:S(2)}) async-start(f32[4,1,32768]{2,1,0:T(1,128)} %reshape.408), calls=%async_computation.1 | async-start | bytes 1048576 | tf_op jit(solution)/shard_map/all_to_all | solution.py:98
  74.0 1.4 gather_fusion.5
  76.6 1.6 fusion.68
  78.1 1.5 fusion.70
  79.7 6.6 %all-to-all-done.1 = f32[4,1,32768]{2,1,0:T(1,128)} async-done(((f32[4,1,32768]{2,1,0:T(1,128)}), f32[4,1,32768]{2,1,0:T(1,128)}, u32[]{:S(2)}, u32[]{:S(2)}) %all-to-all-start.1) | async-done | bytes 524320 | tf_op jit(solution)/shard_map/all_to_all | solution.py:98
  86.3 3.1 %reduce.1 = f32[4,32768]{1,0:T(4,128)S(1)} reduce(f32[4,1,32768]{2,1,0:T(1,128)} %all-to-all-done.1, f32[]{:T(128)} %broadcast.622), dimensions={1}, to_apply=%all_to_all.33.reduce_sub_computation | reduce | bytes 1048580 | tf_op jit(solution)/shard_map/all_to_all | solution.py:98
  92.1 2.4 %fusion.49 = f32[4,2,64,256]{3,2,1,0:T(8,128)S(1)} fusion(f32[4,2,64,256]{3,2,1,0:T(8,128)S(1)} %all_to_all.36, f32[4,1,64,256]{3,2,1,0:T(8,128)S(1)} %copy-done.29, f32[4,1,64,256]{3,2,1,0:T(8,128)S(1)} %copy-done.28, f32[4,1,64,256]{3,2,1,0:T(8,128)} %get-tuple-element.43, f32[4,1,64,256]{3,2,1,0:T(8,128)S(1)} %copy-done.30, ...), kind=kOutput, calls=%fused_computation.59 | convolution fusion | flops 1210056704 | bytes 3407872 | tf_op jit(solution)/shard_map/scij,jk->scik/dot_general | solution.py:94
  95.1 1.4 reshape.410
  96.5 3.5 %all-to-all-start.2 = ((f32[4,1,32768]{2,1,0:T(1,128)}), f32[4,1,32768]{2,1,0:T(1,128)S(1)}, u32[]{:S(2)}, u32[]{:S(2)}) async-start(f32[4,1,32768]{2,1,0:T(1,128)} %reshape.410), calls=%async_computation.2 | async-start | bytes 1048576 | tf_op jit(solution)/shard_map/all_to_all | solution.py:82
  100.1 1.9 %collective-permute-start.7 = (f32[2,2,64,256]{3,2,1,0:T(8,128)S(1)}, f32[2,2,64,256]{3,2,1,0:T(8,128)S(1)}, u32[]{:S(2)}, u32[]{:S(2)}) collective-permute-start(f32[2,2,64,256]{3,2,1,0:T(8,128)S(1)} %get-tuple-element.55), channel_id=1, source_target_pairs={{4,0},{8,4},{12,8},{16,12},{20,16},{24,20},{28,24},{5,1},{9,5},{13... | collective-permute-start | bytes 786440 | tf_op jit(solution)/shard_map/ppermute | solution.py:13
  102.0 4.5 %collective-permute-start.6 = (f32[2,2,64,256]{3,2,1,0:T(8,128)S(1)}, f32[2,2,64,256]{3,2,1,0:T(8,128)S(1)}, u32[]{:S(2)}, u32[]{:S(2)}) collective-permute-start(f32[2,2,64,256]{3,2,1,0:T(8,128)S(1)} %get-tuple-element.54), channel_id=1, source_target_pairs={{0,4},{4,8},{8,12},{12,16},{16,20},{20,24},{24,28},{1,5},{5,9},{9,... | collective-permute-start | bytes 786440 | tf_op jit(solution)/shard_map/ppermute | solution.py:13
  106.5 3.4 %collective-permute-done.7 = f32[2,2,64,256]{3,2,1,0:T(8,128)S(1)} collective-permute-done((f32[2,2,64,256]{3,2,1,0:T(8,128)S(1)}, f32[2,2,64,256]{3,2,1,0:T(8,128)S(1)}, u32[]{:S(2)}, u32[]{:S(2)}) %collective-permute-start.7) | collective-permute-done | bytes 262176 | tf_op jit(solution)/shard_map/ppermute | solution.py:13
  111.4 3.5 %all-to-all-done.2 = f32[4,1,32768]{2,1,0:T(1,128)S(1)} async-done(((f32[4,1,32768]{2,1,0:T(1,128)}), f32[4,1,32768]{2,1,0:T(1,128)S(1)}, u32[]{:S(2)}, u32[]{:S(2)}) %all-to-all-start.2) | async-done | bytes 524320 | tf_op jit(solution)/shard_map/all_to_all | solution.py:82
  114.9 3.0 %reduce.2 = f32[4,32768]{1,0:T(4,128)} reduce(f32[4,1,32768]{2,1,0:T(1,128)S(1)} %all-to-all-done.2, f32[]{:T(128)} %broadcast.622), dimensions={1}, to_apply=%all_to_all.37.reduce_sub_computation | reduce | bytes 1048580 | tf_op jit(solution)/shard_map/all_to_all | solution.py:82
  117.9 1.6 reshape.411
  120.8 2.6 %reshape.227 = f32[4,2,256,64]{2,3,1,0:T(8,128)} reshape(f32[4,2,4,64,64]{3,2,4,1,0:T(4,128)} %copy.25) | data formatting | bytes 1048576 | tf_op jit(solution)/shard_map/reshape | solution.py:81
  123.4 1.7 constant_dynamic-slice_fusion
  125.1 3.4 %collective-permute-start.4 = (f32[2,2,256,64]{2,3,1,0:T(8,128)}, f32[2,2,256,64]{2,3,1,0:T(8,128)}, u32[]{:S(2)}, u32[]{:S(2)}) collective-permute-start(f32[2,2,256,64]{2,3,1,0:T(8,128)} %constant_dynamic-slice_fusion), channel_id=1, source_target_pairs={{0,4},{4,8},{8,12},{12,16},{16,20},{20,24},{24,28},{1,5},{5,9},{9,... | collective-permute-start | bytes 786440 | tf_op jit(solution)/shard_map/ppermute | solution.py:13
  128.5 2.0 %select_multiply_fusion.1 = f32[4,2,64,256]{3,2,1,0:T(8,128)} fusion(f32[4,2,64,256]{3,2,1,0:T(8,128)} %gather_fusion.14, f32[4]{0:T(128)S(1)} %get-tuple-element.81, pred[4]{0:T(512)(128)(4,1)S(1)} %get-tuple-element.76), kind=kLoop, calls=%fused_computation.74 | loop fusion | flops 262144 | bytes 1048596 | tf_op jit(solution)/shard_map/mul | solution.py:70
  134.4 2.1 %collective-permute-start.5 = (f32[2,2,256,64]{2,3,1,0:T(8,128)S(1)}, f32[2,2,256,64]{2,3,1,0:T(8,128)}, u32[]{:S(2)}, u32[]{:S(2)}) collective-permute-start(f32[2,2,256,64]{2,3,1,0:T(8,128)S(1)} %slice.226), channel_id=1, source_target_pairs={{4,0},{8,4},{12,8},{16,12},{20,16},{24,20},{28,24},{5,1},{9,5},{13... | collective-permute-start | bytes 786440 | tf_op jit(solution)/shard_map/ppermute | solution.py:13
  140.9 2.2 %collective-permute-done.5 = f32[2,2,256,64]{2,3,1,0:T(8,128)} collective-permute-done((f32[2,2,256,64]{2,3,1,0:T(8,128)S(1)}, f32[2,2,256,64]{2,3,1,0:T(8,128)}, u32[]{:S(2)}, u32[]{:S(2)}) %collective-permute-start.5) | collective-permute-done | bytes 262176 | tf_op jit(solution)/shard_map/ppermute | solution.py:13
  144.1 1.4 gather_fusion.10
  153.5 1.4 fusion.65
  155.0 2.2 %fusion.40 = f32[4,2,256,64]{2,3,1,0:T(8,128)} fusion(f32[4,1,256,64]{2,3,1,0:T(8,128)S(1)} %get-tuple-element.41, f32[4,1,256,64]{2,3,1,0:T(8,128)S(1)} %get-tuple-element.40, f32[4,1,256,64]{2,3,1,0:T(8,128)S(1)} %get-tuple-element.39, f32[4,1,256,64]{2,3,1,0:T(8,128)S(1)} %get-tuple-element.38, f32[4,2,256,64]{2,3,1,0:T(8,128)S(1)} %copy-done.6, ...), kind=kOutput, calls=%fused_computation.56 | convolution fusion | flops 1209925632 | bytes 2883584 | tf_op jit(solution)/shard_map/ij,scjk->scik/dot_general | solution.py:97
  157.2 1.7 copy.27
  158.9 1.9 %reshape.412 = f32[4,1,32768]{2,1,0:T(1,128)} reshape(f32[256,4,2,64]{3,2,1,0:T(2,128)S(1)} %bitcast.72) | data formatting | bytes 1048576
  160.8 4.3 %all-to-all-start.3 = ((f32[4,1,32768]{2,1,0:T(1,128)}), f32[4,1,32768]{2,1,0:T(1,128)}, u32[]{:S(2)}, u32[]{:S(2)}) async-start(f32[4,1,32768]{2,1,0:T(1,128)} %reshape.412), calls=%async_computation.3 | async-start | bytes 1048576 | tf_op jit(solution)/shard_map/all_to_all | solution.py:98
  168.6 1.6 fusion.59
  170.2 1.5 fusion.61
  171.7 7.2 %all-to-all-done.3 = f32[4,1,32768]{2,1,0:T(1,128)} async-done(((f32[4,1,32768]{2,1,0:T(1,128)}), f32[4,1,32768]{2,1,0:T(1,128)}, u32[]{:S(2)}, u32[]{:S(2)}) %all-to-all-start.3) | async-done | bytes 524320 | tf_op jit(solution)/shard_map/all_to_all | solution.py:98
  178.9 3.1 %reduce.3 = f32[4,32768]{1,0:T(4,128)S(1)} reduce(f32[4,1,32768]{2,1,0:T(1,128)} %all-to-all-done.3, f32[]{:T(128)} %broadcast.622), dimensions={1}, to_apply=%all_to_all.38.reduce_sub_computation | reduce | bytes 1048580 | tf_op jit(solution)/shard_map/all_to_all | solution.py:98
  184.5 2.6 %fusion.46 = f32[4,2,64,256]{3,2,1,0:T(8,128)S(1)} fusion(f32[4,2,64,256]{3,2,1,0:T(8,128)S(1)} %all_to_all.41, f32[4,1,64,256]{3,2,1,0:T(8,128)} %get-tuple-element.37, f32[4,1,64,256]{3,2,1,0:T(8,128)S(1)} %copy-done.27, f32[4,1,64,256]{3,2,1,0:T(8,128)} %get-tuple-element.35, f32[4,1,64,256]{3,2,1,0:T(8,128)} %get-tuple-element.34, ...), kind=kOutput, calls=%fused_computation.58 | convolution fusion | flops 1210056704 | bytes 3407872 | tf_op jit(solution)/shard_map/scij,jk->scik/dot_general | solution.py:94
  (165 shorter events, 57.5 us)
Async XLA Ops:
  1.5 6.2 %copy-start.31 = (s32[8]{0:T(128)S(1)}, s32[8]{0:T(128)}, u32[]{:S(2)}) copy-start(s32[8]{0:T(128)} %param.15) | copy-start | bytes 100
  1.5 8.3 %copy-start = (f32[4,2,64,256]{3,2,1,0:T(8,128)S(1)}, f32[4,2,64,256]{3,2,1,0:T(8,128)}, u32[]{:S(2)}) copy-start(f32[4,2,64,256]{3,2,1,0:T(8,128)} %param.10) | copy-start | bytes 1572868
  3.0 15.7 %copy-start.33 = (f32[2]{0:T(128)S(1)}, f32[2]{0:T(128)}, u32[]{:S(2)}) copy-start(f32[2]{0:T(128)} %param.13) | copy-start | bytes 28
  3.0 18.2 %copy-start.20 = (f32[2,256,256]{2,1,0:T(8,128)S(1)}, f32[2,256,256]{2,1,0:T(8,128)}, u32[]{:S(2)}) copy-start(f32[2,256,256]{2,1,0:T(8,128)} %param.12) | copy-start | bytes 1572868
  3.0 22.5 %all-to-all-start = ((f32[4,1,32768]{2,1,0:T(1,128)}), f32[4,1,32768]{2,1,0:T(1,128)S(1)}, u32[]{:S(2)}, u32[]{:S(2)}) async-start(f32[4,1,32768]{2,1,0:T(1,128)} %reshape.406), calls=%async_computation | async-start | bytes 1048576 | tf_op jit(solution)/shard_map/all_to_all | solution.py:82
  9.9 12.2 %copy-start.32 = (f32[2,2]{1,0:T(2,128)S(1)}, f32[2,2]{1,0:T(2,128)}, u32[]{:S(2)}) copy-start(f32[2,2]{1,0:T(2,128)} %param.14) | copy-start | bytes 52
  9.9 14.0 %collective-permute-start.2 = (f32[2,2,64,256]{3,2,1,0:T(8,128)S(1)}, f32[2,2,64,256]{3,2,1,0:T(8,128)S(1)}, u32[]{:S(2)}, u32[]{:S(2)}) collective-permute-start(f32[2,2,64,256]{3,2,1,0:T(8,128)S(1)} %get-tuple-element.61), channel_id=1, source_target_pairs={{0,4},{4,8},{8,12},{12,16},{16,20},{20,24},{24,28},{1,5},{5,9},{9,... | collective-permute-start | bytes 786440 | tf_op jit(solution)/shard_map/ppermute | solution.py:13
  13.9 10.1 %collective-permute-start.3 = (f32[2,2,64,256]{3,2,1,0:T(8,128)S(1)}, f32[2,2,64,256]{3,2,1,0:T(8,128)S(1)}, u32[]{:S(2)}, u32[]{:S(2)}) collective-permute-start(f32[2,2,64,256]{3,2,1,0:T(8,128)S(1)} %get-tuple-element.60), channel_id=1, source_target_pairs={{4,0},{8,4},{12,8},{16,12},{20,16},{24,20},{28,24},{5,1},{9,5},{13... | collective-permute-start | bytes 786440 | tf_op jit(solution)/shard_map/ppermute | solution.py:13
  31.9 16.5 %copy-start.7 = (f32[4,2,256,64]{2,3,1,0:T(8,128)}, f32[4,2,256,64]{2,3,1,0:T(8,128)S(1)}, u32[]{:S(2)}) copy-start(f32[4,2,256,64]{2,3,1,0:T(8,128)S(1)} %reshape.223) | copy-start | bytes 1572868
  32.7 14.7 %collective-permute-start = (f32[2,2,256,64]{2,3,1,0:T(8,128)}, f32[2,2,256,64]{2,3,1,0:T(8,128)}, u32[]{:S(2)}, u32[]{:S(2)}) collective-permute-start(f32[2,2,256,64]{2,3,1,0:T(8,128)} %constant_dynamic-slice_fusion.2), channel_id=1, source_target_pairs={{0,4},{4,8},{8,12},{12,16},{16,20},{20,24},{24,28},{1,5},{5,9},{9,... | collective-permute-start | bytes 786440 | tf_op jit(solution)/shard_map/ppermute | solution.py:13
  41.5 3.6 %copy-start.18 = (f32[4,2,64,256]{3,2,1,0:T(8,128)S(1)}, f32[4,2,64,256]{3,2,1,0:T(8,128)}, u32[]{:S(2)}) copy-start(f32[4,2,64,256]{3,2,1,0:T(8,128)} %gather_fusion.7) | copy-start | bytes 1572868
  43.1 8.7 %collective-permute-start.1 = (f32[2,2,256,64]{2,3,1,0:T(8,128)S(1)}, f32[2,2,256,64]{2,3,1,0:T(8,128)}, u32[]{:S(2)}, u32[]{:S(2)}) collective-permute-start(f32[2,2,256,64]{2,3,1,0:T(8,128)S(1)} %slice.195), channel_id=1, source_target_pairs={{4,0},{8,4},{12,8},{16,12},{20,16},{24,20},{28,24},{5,1},{9,5},{13... | collective-permute-start | bytes 786440 | tf_op jit(solution)/shard_map/ppermute | solution.py:13
  56.2 2.0 %copy-start.5 = (f32[4,2,256,64]{2,3,1,0:T(8,128)S(1)}, f32[4,2,256,64]{2,3,1,0:T(8,128)}, u32[]{:S(2)}) copy-start(f32[4,2,256,64]{2,3,1,0:T(8,128)} %gather_fusion.3) | copy-start | bytes 1572868
  60.5 1.0 copy-start.4
  60.5 1.2 copy-start.14
  60.5 1.4 copy-start.15
  63.3 1.5 copy-start.8
  63.3 1.5 copy-start.21
  63.3 1.5 copy-start.23
  63.3 1.5 copy-start.34
  68.9 4.9 %copy-start.17 = (f32[4,2,64,256]{3,2,1,0:T(8,128)S(1)}, f32[4,2,64,256]{3,2,1,0:T(8,128)}, u32[]{:S(2)}) copy-start(f32[4,2,64,256]{3,2,1,0:T(8,128)} %gather_fusion.4) | copy-start | bytes 1572868
  68.9 17.4 %all-to-all-start.1 = ((f32[4,1,32768]{2,1,0:T(1,128)}), f32[4,1,32768]{2,1,0:T(1,128)}, u32[]{:S(2)}, u32[]{:S(2)}) async-start(f32[4,1,32768]{2,1,0:T(1,128)} %reshape.408), calls=%async_computation.1 | async-start | bytes 1048576 | tf_op jit(solution)/shard_map/all_to_all | solution.py:98
  74.0 2.6 %copy-start.11 = (f32[4,2,64,256]{3,2,1,0:T(8,128)S(1)}, f32[4,2,64,256]{3,2,1,0:T(8,128)}, u32[]{:S(2)}) copy-start(f32[4,2,64,256]{3,2,1,0:T(8,128)} %select_multiply_fusion.9) | copy-start | bytes 1572868
  74.0 2.6 %copy-start.12 = (f32[4,2,64,256]{3,2,1,0:T(8,128)S(1)}, f32[4,2,64,256]{3,2,1,0:T(8,128)}, u32[]{:S(2)}) copy-start(f32[4,2,64,256]{3,2,1,0:T(8,128)} %select_multiply_fusion.8) | copy-start | bytes 1572868
  90.9 1.0 copy-start.24
  90.9 1.0 copy-start.28
  90.9 1.1 copy-start.29
  90.9 1.2 copy-start.30
  96.5 18.4 %all-to-all-start.2 = ((f32[4,1,32768]{2,1,0:T(1,128)}), f32[4,1,32768]{2,1,0:T(1,128)S(1)}, u32[]{:S(2)}, u32[]{:S(2)}) async-start(f32[4,1,32768]{2,1,0:T(1,128)} %reshape.410), calls=%async_computation.2 | async-start | bytes 1048576 | tf_op jit(solution)/shard_map/all_to_all | solution.py:82
  100.1 9.8 %collective-permute-start.7 = (f32[2,2,64,256]{3,2,1,0:T(8,128)S(1)}, f32[2,2,64,256]{3,2,1,0:T(8,128)S(1)}, u32[]{:S(2)}, u32[]{:S(2)}) collective-permute-start(f32[2,2,64,256]{3,2,1,0:T(8,128)S(1)} %get-tuple-element.55), channel_id=1, source_target_pairs={{4,0},{8,4},{12,8},{16,12},{20,16},{24,20},{28,24},{5,1},{9,5},{13... | collective-permute-start | bytes 786440 | tf_op jit(solution)/shard_map/ppermute | solution.py:13
  102.0 7.9 %collective-permute-start.6 = (f32[2,2,64,256]{3,2,1,0:T(8,128)S(1)}, f32[2,2,64,256]{3,2,1,0:T(8,128)S(1)}, u32[]{:S(2)}, u32[]{:S(2)}) collective-permute-start(f32[2,2,64,256]{3,2,1,0:T(8,128)S(1)} %get-tuple-element.54), channel_id=1, source_target_pairs={{0,4},{4,8},{8,12},{12,16},{16,20},{20,24},{24,28},{1,5},{5,9},{9,... | collective-permute-start | bytes 786440 | tf_op jit(solution)/shard_map/ppermute | solution.py:13
  125.1 13.8 %collective-permute-start.4 = (f32[2,2,256,64]{2,3,1,0:T(8,128)}, f32[2,2,256,64]{2,3,1,0:T(8,128)}, u32[]{:S(2)}, u32[]{:S(2)}) collective-permute-start(f32[2,2,256,64]{2,3,1,0:T(8,128)} %constant_dynamic-slice_fusion), channel_id=1, source_target_pairs={{0,4},{4,8},{8,12},{12,16},{16,20},{20,24},{24,28},{1,5},{5,9},{9,... | collective-permute-start | bytes 786440 | tf_op jit(solution)/shard_map/ppermute | solution.py:13
  132.7 3.8 %copy-start.19 = (f32[4,2,64,256]{3,2,1,0:T(8,128)S(1)}, f32[4,2,64,256]{3,2,1,0:T(8,128)}, u32[]{:S(2)}) copy-start(f32[4,2,64,256]{3,2,1,0:T(8,128)} %gather_fusion.15) | copy-start | bytes 1572868
  134.4 8.7 %collective-permute-start.5 = (f32[2,2,256,64]{2,3,1,0:T(8,128)S(1)}, f32[2,2,256,64]{2,3,1,0:T(8,128)}, u32[]{:S(2)}, u32[]{:S(2)}) collective-permute-start(f32[2,2,256,64]{2,3,1,0:T(8,128)S(1)} %slice.226), channel_id=1, source_target_pairs={{4,0},{8,4},{12,8},{16,12},{20,16},{24,20},{28,24},{5,1},{9,5},{13... | collective-permute-start | bytes 786440 | tf_op jit(solution)/shard_map/ppermute | solution.py:13
  149.6 1.3 copy-start.1
  149.6 1.4 copy-start.2
  150.9 1.1 copy-start.3
  153.5 1.5 copy-start.6
  153.5 1.5 copy-start.22
  153.5 1.5 copy-start.25
  153.5 1.5 copy-start.35
  160.8 4.3 %copy-start.16 = (f32[4,2,64,256]{3,2,1,0:T(8,128)S(1)}, f32[4,2,64,256]{3,2,1,0:T(8,128)}, u32[]{:S(2)}) copy-start(f32[4,2,64,256]{3,2,1,0:T(8,128)} %gather_fusion.12) | copy-start | bytes 1572868
  160.8 18.1 %all-to-all-start.3 = ((f32[4,1,32768]{2,1,0:T(1,128)}), f32[4,1,32768]{2,1,0:T(1,128)}, u32[]{:S(2)}, u32[]{:S(2)}) async-start(f32[4,1,32768]{2,1,0:T(1,128)} %reshape.412), calls=%async_computation.3 | async-start | bytes 1048576 | tf_op jit(solution)/shard_map/all_to_all | solution.py:98
  166.0 2.6 %copy-start.9 = (f32[4,2,64,256]{3,2,1,0:T(8,128)S(1)}, f32[4,2,64,256]{3,2,1,0:T(8,128)}, u32[]{:S(2)}) copy-start(f32[4,2,64,256]{3,2,1,0:T(8,128)} %select_multiply_fusion.1) | copy-start | bytes 1572868
  166.0 2.6 %copy-start.10 = (f32[4,2,64,256]{3,2,1,0:T(8,128)S(1)}, f32[4,2,64,256]{3,2,1,0:T(8,128)}, u32[]{:S(2)}) copy-start(f32[4,2,64,256]{3,2,1,0:T(8,128)} %select_multiply_fusion) | copy-start | bytes 1572868
  168.6 1.6 copy-start.13
  183.5 1.0 copy-start.26
  183.5 1.0 copy-start.27
